TPU v7x, 256 devices: a whole 4x4x8 slice. The times are simulated.
256 devices in a mesh: seq: 64 (over z, x, core), vol: 4 (over y).
Axes of the slice: x: 4, y: 4, z: 8, core: 2. Of those that a mesh axis runs over, the one named last changes fastest.
Arguments:
- x_raw: bfloat16 [65536, 4096], P(('vol', 'seq')), parts along dimension 0, may hold values from -6 to 6
- z_gate: bfloat16 [65536, 4096], P(('vol', 'seq')), parts along dimension 0, may hold values from -6 to 6
- bc_raw: bfloat16 [65536, 256], P(('vol', 'seq')), parts along dimension 0, may hold values from -6 to 6
- dt_raw: bfloat16 [65536, 64], P(('vol', 'seq')), parts along dimension 0, may hold values from -5 to 5
- conv_x: float32 [4, 4096], replicated, may hold values from -3 to 3
- conv_x_bias: float32 [4096], replicated, may hold values from -0.5 to 0.5
- conv_bc: float32 [4, 256], replicated, may hold values from -3 to 3
- conv_bc_bias: float32 [256], replicated, may hold values from -0.5 to 0.5
- dt_bias: float32 [64], replicated, may hold values from -3 to 0
- a_log: float32 [64], replicated, may hold values from -11 to -2
- skip_gain: float32 [64], replicated, may hold values from 0.5 to 1.5
- norm_gain: float32 [4096], replicated, may hold values from 0.5 to 1.5
Outputs:
- mixed: bfloat16 [65536, 4096], P(('vol', 'seq')), parts along dimension 0
There are 4 independent parts, one for each index of `vol`. A program takes and returns all parts, laid end to end along the dimension named above; an argument that names none is the same for every part. Nothing has to cross between parts.
All inputs are finite; a program needn't handle non-finite values.
Results may differ from a plain program's by a relative error of at most 0.0055.
Values may be sent and summed in bfloat16 or wider, within the bound.
A program may use at most 192 MiB of HBM per device.

v0:
```python
import functools

import jax
import jax.numpy as jnp
from jax import lax
from jax.experimental import pallas as pl
from jax.experimental.pallas import tpu as pltpu
from jax.sharding import PartitionSpec as P

T = 256
N = 128
HL = 64
LOG2E = 1.4426950408889634
F32 = jnp.float32
BF16 = jnp.bfloat16


def dot(a, b):
    return jnp.dot(a, b, preferred_element_type=F32)


def silu(v):
    return v / (1.0 + jnp.exp(-v))


def kernel(
    nz,
    nx,
    di,
    nk,
    x_hbm,
    z_hbm,
    bc_ref,
    dt_ref,
    wx_ref,
    bx_ref,
    wbc_ref,
    bbc_ref,
    dtb_ref,
    alog_ref,
    skip_ref,
    gain_ref,
    out_hbm,
    xv,
    zv,
    xc,
    halo_x,
    halo_bc,
    dtw,
    ex,
    ldg,
    rt,
    f1s,
    f2s,
    bt,
    cm,
    sc,
    skw,
    inside,
    ssq,
    ov,
    lo_b,
    lp_b,
    cl_b,
    xd_b,
    pl_b,
    zd_b,
    dx,
    dl,
    dz,
    sbf,
    srecv,
    csb,
    xrecv,
    ptb,
    zrecv,
    pesend,
    perecv,
    esend,
    erecv,
    entsend,
    ent,
    sem_in,
    sem_out,
    sem_halo,
    sem_l,
    sx_s,
    sx_r,
    sz_s,
    sz_r,
    d_s,
    d_r,
    x_s,
    x_r,
    z_s,
    z_r,
    zb_s,
    zb_r,
    xb_s,
    xb_r,
    db_s,
    db_r,
):
    ch = di // nk
    zw = ch // nz
    hr = N // 2
    xr = hr // nx
    ngroup = di // 512

    me = lax.axis_index("seq")
    c = lax.rem(me, 2)
    x = lax.rem(me // 2, nx)
    z = me // (2 * nx)
    nseq = 2 * nx * nz

    def at(zz, xx, cc):
        return (zz * nx + xx) * 2 + cc

    partner = at(z, x, 1 - c)
    nxt = lax.rem(me + 1, nseq)
    prv = lax.rem(me + nseq - 1, nseq)
    xpeer = [lax.rem(x + d, nx) for d in range(1, nx)]
    zpeer = [lax.rem(z + d, nz) for d in range(1, nz)]

    barrier = pltpu.get_barrier_semaphore()
    peers = [partner, nxt, prv]
    peers += [at(z, xp, c) for xp in xpeer]
    peers += [at(zp, x, c) for zp in zpeer]
    for p in peers:
        pl.semaphore_signal(barrier, inc=1, device_id={"seq": p})

    def rcopy(src, dst, ss, rs, dev):
        return pltpu.make_async_remote_copy(
            src_ref=src, dst_ref=dst, send_sem=ss, recv_sem=rs, device_id={"seq": dev}
        )

    half = di // 2
    cols = [pl.ds(0, half), pl.ds(half, half)]
    xin = [pltpu.make_async_copy(x_hbm.at[:, q], xv.at[:, q], sem_in.at[i]) for i, q in enumerate(cols)]
    zin = pltpu.make_async_copy(z_hbm, zv, sem_in.at[2])
    for cp in xin:
        cp.start()
    zin.start()

    dtw[:, 0:HL] = dt_ref[...].astype(F32) + dtb_ref[...]
    dtw[:, HL : 2 * HL] = dt_ref[...].astype(F32) + dtb_ref[...]
    lo_b[:, 0:HL] = jnp.broadcast_to(jnp.exp(alog_ref[...]), (8, HL))
    lo_b[:, HL : 2 * HL] = jnp.broadcast_to(jnp.exp(alog_ref[...]), (8, HL))
    arate = lo_b[0:1, :]
    lo_b[:, 0:HL] = jnp.broadcast_to(skip_ref[...], (8, HL))
    lo_b[:, HL : 2 * HL] = jnp.broadcast_to(skip_ref[...], (8, HL))
    skipd = lo_b[...]
    raw = dtw[...]
    step = jnp.maximum(raw, 0.0) + jnp.log1p(jnp.exp(-jnp.abs(raw)))
    rate = -arate * step
    low = lax.broadcasted_iota(jnp.int32, (T, T), 0) >= lax.broadcasted_iota(jnp.int32, (T, T), 1)
    ld2 = jnp.dot(
        jnp.where(low, 1.0, 0.0),
        rate,
        precision=lax.Precision.HIGHEST,
        preferred_element_type=F32,
    ) * LOG2E
    r2 = ld2 - jnp.log(step) * LOG2E
    last2 = ld2[T - 1 : T, :]

    def pair(v):
        hi = v.astype(BF16).astype(F32)
        lane = lax.broadcasted_iota(jnp.int32, v.shape, 1)
        return jnp.where(lane < HL, hi, v - hi).astype(BF16)

    f1s[...] = pair(jnp.exp2(last2 - r2))
    f2s[...] = pair(jnp.exp2(ld2))
    rt[...] = jnp.transpose(r2)
    for g in range(ngroup):
        ldg[g] = ld2 if g == 0 else pltpu.roll(ld2, 128 - 8 * g, axis=1)
    lo_b[...] = jnp.broadcast_to(last2, (8, 2 * HL))

    @pl.loop(0, ngroup)
    def _(g):
        row = lax.broadcasted_iota(jnp.int32, (128, 512), 0) & 63
        head = (lax.broadcasted_iota(jnp.int32, (128, 512), 1) >> 6) + g * 8
        lanes = pl.ds(pl.multiple_of(g * 512, 512), 512)
        ex[:, lanes] = jnp.where(row == head, 1.0, 0.0).astype(BF16)
        skw[:, lanes] = dot(pair(jnp.concatenate([skipd, skipd], 0)), ex[:, lanes])[0:8]

    pl.semaphore_wait(barrier, len(peers))
    hal = [
        rcopy(x_hbm.at[pl.ds(T - 8, 8), :], halo_x, sem_halo.at[0], sem_halo.at[1], nxt),
        rcopy(bc_ref.at[pl.ds(T - 8, 8), :], halo_bc, sem_halo.at[2], sem_halo.at[3], nxt),
    ]
    for cp in hal:
        cp.start()
    lcopy = rcopy(lo_b, lp_b, sem_l.at[0], sem_l.at[1], partner)
    lcopy.start()

    def conv_main(src, dst, w_ref, b_ref, lanes):
        v = src[:, lanes].astype(F32)
        acc = b_ref[:, lanes] + w_ref[3:4, lanes] * v
        for k in range(1, 4):
            acc = acc + w_ref[3 - k : 4 - k, lanes] * pltpu.roll(v, k, axis=0)
        dst[:, lanes] = silu(acc).astype(BF16)

    def conv_head(src, halo, w_ref, b_ref, lanes):
        top = jnp.where(me > 0, halo[:, lanes].astype(F32), 0.0)
        v = jnp.concatenate([top, src[0:16, lanes].astype(F32)], axis=0)
        acc = b_ref[:, lanes] + w_ref[3:4, lanes] * v
        for k in range(1, 4):
            acc = acc + w_ref[3 - k : 4 - k, lanes] * pltpu.roll(v, k, axis=0)
        return silu(acc[8:24]).astype(BF16)

    for i in range(2):
        xin[i].wait()

        @pl.loop(0, half // 256)
        def _(j):
            conv_main(xv, xc, wx_ref, bx_ref, pl.ds(pl.multiple_of(i * half + j * 256, 256), 256))

    for cp in hal:
        cp.wait_recv()

    @pl.loop(0, di // 512)
    def _(j):
        lanes = pl.ds(pl.multiple_of(j * 512, 512), 512)
        xc[0:16, lanes] = conv_head(xv, halo_x, wx_ref, bx_ref, lanes)

    whole = pl.ds(0, 2 * N)
    bcs = ov.at[:, pl.ds(0, 2 * N)]
    conv_main(bc_ref, bcs, wbc_ref, bbc_ref, whole)
    bcs[0:16, :] = conv_head(bc_ref, halo_bc, wbc_ref, bbc_ref, whole)
    bm = bcs[:, 0:N]
    cm[...] = bcs[:, N : 2 * N]
    bt[...] = jnp.transpose(bm.astype(F32)).astype(BF16)

    lcopy.wait_recv()
    own = lo_b[...]
    other = lp_b[...]
    first = c == 0
    l0 = jnp.where(first, own, other)
    l1 = jnp.where(first, other, own)
    cl = l0 + l1
    cl_b[...] = cl
    xd_b[x] = cl
    dxs = [rcopy(cl_b, xd_b.at[x], sx_s.at[d], sx_r.at[x], at(z, xp, c)) for d, xp in enumerate(xpeer)]
    for cp in dxs:
        cp.start()
    dl[...] = dot(
        pair(jnp.concatenate([jnp.exp2(l0), jnp.exp2(l1)], axis=0)), ex[...]
    )

    def lanes_of(k):
        return pl.ds(k * ch, ch)

    oh = pl.multiple_of(c * hr, hr)
    ph = pl.multiple_of((1 - c) * hr, hr)

    def d_copy(k):
        return rcopy(
            sbf.at[pl.ds(ph, hr), lanes_of(k)], srecv.at[:, lanes_of(k)], d_s.at[k], d_r.at[k], partner
        )

    def stage_a(k):
        for j in range(ch // 256):
            lanes = pl.ds(k * ch + j * 256, 256)
            f1e = dot(f1s[...], ex[:, lanes])
            weighted = (xc[:, lanes].astype(F32) * f1e).astype(BF16)
            sbf[:, lanes] = dot(bt[...], weighted).astype(BF16)
        d_copy(k).start()

    def x_copy(k, d):
        xp = xpeer[d]
        rows = pl.ds(pl.multiple_of(xp * xr, xr), xr)
        return rcopy(
            csb.at[rows, lanes_of(k)],
            xrecv.at[x, :, lanes_of(k)],
            x_s.at[k, d],
            x_r.at[k, x],
            at(z, xp, c),
        )

    def x_wait(k, d):
        xp = xpeer[d]
        rcopy(
            csb.at[pl.ds(0, xr), lanes_of(k)],
            xrecv.at[xp, :, lanes_of(k)],
            x_s.at[k, d],
            x_r.at[k, xp],
            at(z, xp, c),
        ).wait_recv()

    def stage_b(k):
        d_copy(k).wait_recv()
        lanes = lanes_of(k)
        mine = sbf[pl.ds(oh, hr), lanes].astype(F32)
        got = srecv[:, lanes].astype(F32)
        e1 = dl[8:9, lanes]
        wm = jnp.where(first, e1, 1.0)
        wg = jnp.where(first, 1.0, e1)
        csb[:, lanes] = (wm * mine + wg * got).astype(BF16)
        for d in range(nx - 1):
            x_copy(k, d).start()
        xrecv[x, :, lanes] = csb[pl.ds(pl.multiple_of(x * xr, xr), xr), lanes]

    def stage_decay_x():
        for d, xp in enumerate(xpeer):
            rcopy(cl_b, xd_b.at[xp], sx_s.at[d], sx_r.at[xp], at(z, xp, c)).wait_recv()
        rows = [xd_b[i][0:1] for i in range(nx)]
        total = rows[0]
        for i in range(1, nx):
            total = total + rows[i]
        after = []
        run = jnp.zeros_like(rows[0])
        for i in reversed(range(nx)):
            after.insert(0, run)
            run = run + rows[i]
        full = jnp.concatenate(
            after + rows + [jnp.zeros_like(rows[0])] * (16 - 2 * nx), axis=0
        )
        dx[...] = dot(pair(jnp.exp2(full)), ex[...])
        pl_b[...] = jnp.broadcast_to(total, (8, 2 * HL))
        zd_b[z] = jnp.broadcast_to(total, (8, 2 * HL))
        for d, zp in enumerate(zpeer):
            rcopy(pl_b, zd_b.at[z], sz_s.at[d], sz_r.at[z], at(zp, x, c)).start()

    def stage_decay_z():
        for d, zp in enumerate(zpeer):
            rcopy(pl_b, zd_b.at[zp], sz_s.at[d], sz_r.at[zp], at(zp, x, c)).wait_recv()
        full = jnp.concatenate(
            [zd_b[i][0:1] for i in range(nz)] + [jnp.zeros((16 - nz, 2 * HL), F32)], axis=0
        )
        full = pair(jnp.exp2(full))
        for k in range(nk):
            lanes = pl.ds(pl.multiple_of(k * ch + z * zw, zw), zw)
            dz[:, k * zw : (k + 1) * zw] = dot(full, ex[:, lanes])

    def z_copy(k, d):
        zp = zpeer[d]
        src = ptb.at[:, pl.ds(pl.multiple_of(k * ch + zp * zw, zw), zw)]
        return rcopy(
            src, zrecv.at[z, :, pl.ds(k * zw, zw)], z_s.at[k, d], z_r.at[k, z], at(zp, x, c)
        )

    def stage_c(k):
        for d in range(nx - 1):
            x_wait(k, d)
        lanes = lanes_of(k)
        tot = dx[0:1, lanes] * xrecv[0, :, lanes].astype(F32)
        for i in range(1, nx):
            tot = tot + dx[i : i + 1, lanes] * xrecv[i, :, lanes].astype(F32)
        ptb[:, lanes] = tot.astype(BF16)
        for d in range(nz - 1):
            z_copy(k, d).start()
        zrecv[z, :, pl.ds(k * zw, zw)] = ptb[:, pl.ds(pl.multiple_of(k * ch + z * zw, zw), zw)]

    def zb_copy(k, d):
        zp = zpeer[d]
        lanes = pl.ds(pl.multiple_of(k * ch + z * zw, zw), zw)
        return rcopy(
            pesend.at[zp, :, pl.ds(k * zw, zw)],
            perecv.at[:, lanes],
            zb_s.at[k, d],
            zb_r.at[k, z],
            at(zp, x, c),
        )

    def stage_d(k):
        own_lanes = pl.ds(k * zw, zw)
        for d, zp in enumerate(zpeer):
            rcopy(
                ptb.at[:, pl.ds(0, zw)],
                zrecv.at[zp, :, own_lanes],
                z_s.at[k, d],
                z_r.at[k, zp],
                at(zp, x, c),
            ).wait_recv()
        state = jnp.zeros((xr, zw), F32)
        for i in range(nz):
            pesend[i, :, own_lanes] = state.astype(BF16)
            state = dz[i : i + 1, own_lanes] * state + zrecv[i, :, own_lanes].astype(F32)
        for d in range(nz - 1):
            zb_copy(k, d).start()
        perecv[:, pl.ds(pl.multiple_of(k * ch + z * zw, zw), zw)] = pesend[z, :, own_lanes]

    def xb_copy(k, d):
        xp = xpeer[d]
        rows = pl.ds(pl.multiple_of(x * xr, xr), xr)
        return rcopy(
            esend.at[xp, :, lanes_of(k)],
            erecv.at[rows, lanes_of(k)],
            xb_s.at[k, d],
            xb_r.at[k, x],
            at(z, xp, c),
        )

    def stage_e(k):
        for d, zp in enumerate(zpeer):
            lanes = pl.ds(pl.multiple_of(k * ch + zp * zw, zw), zw)
            rcopy(
                pesend.at[zp, :, pl.ds(k * zw, zw)],
                perecv.at[:, lanes],
                zb_s.at[k, d],
                zb_r.at[k, zp],
                at(zp, x, c),
            ).wait_recv()
        lanes = lanes_of(k)
        state = perecv[:, lanes].astype(F32)
        for i in range(nx):
            esend[i, :, lanes] = state.astype(BF16)
            if i < nx - 1:
                state = dx[nx + i : nx + i + 1, lanes] * state + xrecv[i, :, lanes].astype(F32)
        for d in range(nx - 1):
            xb_copy(k, d).start()
        erecv[pl.ds(pl.multiple_of(x * xr, xr), xr), lanes] = esend[x, :, lanes]

    def db_copy(k):
        return rcopy(
            entsend.at[:, lanes_of(k)],
            ent.at[pl.ds(oh, hr), lanes_of(k)],
            db_s.at[k],
            db_r.at[k],
            partner,
        )

    def stage_f(k):
        lanes = lanes_of(k)
        for d, xp in enumerate(xpeer):
            rows = pl.ds(pl.multiple_of(xp * xr, xr), xr)
            rcopy(
                esend.at[xp, :, lanes],
                erecv.at[rows, lanes],
                xb_s.at[k, d],
                xb_r.at[k, xp],
                at(z, xp, c),
            ).wait_recv()
        e0 = erecv[:, lanes]
        mine = sbf[pl.ds(oh, hr), lanes]
        got = srecv[:, lanes]
        s0 = jnp.where(first, mine, got).astype(F32)
        e1 = (dl[0:1, lanes] * e0.astype(F32) + s0).astype(BF16)
        entsend[:, lanes] = jnp.where(first, e1, e0)
        db_copy(k).start()
        ent[pl.ds(oh, hr), lanes] = jnp.where(first, e0, e1)

    def scores():
        s = lax.dot_general(
            cm[...], bcs[:, 0:N], (((1,), (1,)), ((), ())), preferred_element_type=F32
        )
        low_mask = lax.broadcasted_iota(jnp.int32, (T, T), 0) >= lax.broadcasted_iota(
            jnp.int32, (T, T), 1
        )
        sc[...] = jnp.where(low_mask, s, 0.0)

    hb = T // 2

    def mix_group(g):
        ldt = ldg[g]
        rtile = rt[pl.ds(pl.multiple_of(g * 8, 8), 8), :]
        for j in range(4):
            lanes = pl.ds(pl.multiple_of(g * 512 + j * 128, 128), 128)
            xp = xc[:, lanes]
            lane = lax.broadcasted_iota(jnp.int32, (T, 128), 1)
            xa = jnp.where(lane < 64, xp.astype(F32), 0.0).astype(BF16)
            xb = jnp.where(lane >= 64, xp.astype(F32), 0.0).astype(BF16)
            tops = []
            bots = []
            for a in range(2):
                i = 2 * j + a
                col = ldt[:, i : i + 1]
                row = rtile[i : i + 1, :]
                tl = jnp.exp2(jnp.minimum(col[0:hb] - row[:, 0:hb], 126.0)) * sc[0:hb, 0:hb]
                bl = jnp.exp2(col[hb:T] - row[:, 0:hb]) * sc[hb:T, 0:hb]
                br = jnp.exp2(jnp.minimum(col[hb:T] - row[:, hb:T], 126.0)) * sc[hb:T, hb:T]
                tops.append(tl.astype(BF16))
                bots += [bl.astype(BF16), br.astype(BF16)]
            yt = dot(jnp.concatenate(tops, 1), jnp.concatenate([xa[0:hb], xb[0:hb]], 0))
            yb = dot(jnp.concatenate(bots, 1), jnp.concatenate([xa, xb], 0))
            sk = skw[0:1, lanes] * xp.astype(F32)
            inside[0:hb, lanes] = yt + sk[0:hb]
            inside[hb:T, lanes] = yb + sk[hb:T]

    def stage_g(k):
        db_copy(k).wait_recv()

        @pl.loop(0, ch // 256)
        def _(j):
            lanes = pl.ds(pl.multiple_of(k * ch + j * 256, 256), 256)
            f2e = dot(f2s[...], ex[:, lanes])
            y = (inside[:, lanes] + f2e * dot(cm[...], ent[:, lanes])).astype(BF16)
            gated = y.astype(F32) * silu(zv[:, lanes].astype(F32))
            inside[:, lanes] = gated
            sq = gated * gated
            ssq[...] += sq[:, 0:128] + sq[:, 128:256]

    stage_a(0)
    stage_a(1)
    stage_b(0)
    for k in range(2, nk):
        stage_a(k)
        stage_b(k - 1)
    stage_decay_x()
    stage_b(nk - 1)
    scores()
    ssq[...] = jnp.zeros_like(ssq)
    zin.wait()

    fill = list(range(ngroup))

    def filler():
        if fill:
            g = fill.pop(0)
            mix_group(g)

    for s in range(nk):
        filler()
        stage_c(s)
    stage_decay_z()
    for s in range(nk):
        filler()
        stage_d(s)
    while fill:
        filler()
    for s in range(nk):
        stage_e(s)
    for s in range(nk):
        stage_f(s)
    for s in range(nk):
        stage_g(s)

    ms = jnp.sum(ssq[...], axis=1, keepdims=True) * (1.0 / di)
    rs = lax.rsqrt(ms + 1e-05)
    outs = []
    for i in range(nk):

        @pl.loop(0, ch // 256)
        def _(j):
            lanes = pl.ds(pl.multiple_of(i * ch + j * 256, 256), 256)
            ov[:, lanes] = (inside[:, lanes] * rs * gain_ref[:, lanes]).astype(BF16)

        cp = pltpu.make_async_copy(ov.at[:, lanes_of(i)], out_hbm.at[:, lanes_of(i)], sem_out.at[i])
        cp.start()
        outs.append(cp)

    for cp in hal:
        cp.wait_send()
    lcopy.wait_send()
    for d in range(nx - 1):
        dxs[d].wait_send()
    for d, zp in enumerate(zpeer):
        rcopy(pl_b, zd_b.at[z], sz_s.at[d], sz_r.at[z], at(zp, x, c)).wait_send()
    for k in range(nk):
        d_copy(k).wait_send()
        db_copy(k).wait_send()
        for d in range(nx - 1):
            x_copy(k, d).wait_send()
            xb_copy(k, d).wait_send()
        for d in range(nz - 1):
            z_copy(k, d).wait_send()
            zb_copy(k, d).wait_send()
    for cp in outs:
        cp.wait()


def make_body(nz, nx, nk):
    def body(x_raw, z_gate, bc_raw, dt_raw, wx, bx, wbc, bbc, dtb, alog, skip, gain):
        di = x_raw.shape[1]
        ch = di // nk
        zw = ch // nz
        hr = N // 2
        xr = hr // nx
        ng = di // 512
        vm = lambda *s: pltpu.VMEM(s, F32)
        vb = lambda *s: pltpu.VMEM(s, BF16)
        dma = lambda *s: pltpu.SemaphoreType.DMA(s)
        anyspec = pl.BlockSpec(memory_space=pl.ANY)
        vspec = pl.BlockSpec(memory_space=pltpu.VMEM)
        scratch = [
            vb(T, di),
            vb(T, di),
            vb(T, di),
            vb(8, di),
            vb(8, 2 * N),
            vm(T, 128),
            vb(128, di),
            vm(ng, T, 128),
            vm(128, T),
            vb(T, 128),
            vb(T, 128),
            vb(N, T),
            vb(T, N),
            vm(T, T),
            vm(8, di),
            vm(T, di),
            vm(T, 128),
            vb(T, di),
            vm(8, 128),
            vm(8, 128),
            vm(8, 128),
            vm(nx, 8, 128),
            vm(8, 128),
            vm(nz, 8, 128),
            vm(16, di),
            vm(16, di),
            vm(16, nk * zw),
            vb(N, di),
            vb(hr, di),
            vb(hr, di),
            vb(nx, xr, di),
            vb(xr, di),
            vb(nz, xr, nk * zw),
            vb(nz, xr, nk * zw),
            vb(xr, di),
            vb(nx, xr, di),
            vb(hr, di),
            vb(hr, di),
            vb(N, di),
            dma(3),
            dma(nk),
            dma(4),
            dma(2),
            dma(nx),
            dma(nx),
            dma(nz),
            dma(nz),
            dma(nk),
            dma(nk),
            dma(nk, nx),
            dma(nk, nx),
            dma(nk, nz),
            dma(nk, nz),
            dma(nk, nz),
            dma(nk, nz),
            dma(nk, nx),
            dma(nk, nx),
            dma(nk),
            dma(nk),
        ]
        return pl.pallas_call(
            functools.partial(kernel, nz, nx, di, nk),
            out_shape=jax.ShapeDtypeStruct((T, di), BF16),
            in_specs=[anyspec, anyspec] + [vspec] * 10,
            out_specs=anyspec,
            scratch_shapes=scratch,
            compiler_params=pltpu.CompilerParams(
                collective_id=0, has_side_effects=True, vmem_limit_bytes=60 * 1024 * 1024
            ),
        )(
            x_raw,
            z_gate,
            bc_raw,
            dt_raw,
            wx,
            bx.reshape(1, -1),
            wbc,
            bbc.reshape(1, -1),
            dtb.reshape(1, -1),
            alog.reshape(1, -1),
            skip.reshape(1, -1),
            gain.reshape(1, -1),
        )

    return body


def solution(mesh):
    nx = 4
    nz = mesh.shape["seq"] // (2 * nx)
    tok = P(("vol", "seq"), None)
    return jax.shard_map(
        make_body(nz, nx, 4),
        mesh=mesh,
        in_specs=(tok, tok, tok, tok) + (P(),) * 8,
        out_specs=tok,
        check_vma=False,
    )
```

profile of v0, /device:TPU:1, one launch (start us, length us, event | category | flops | bytes accessed | tf_op | source)
XLA Modules:
  0.0 49.7 jit_solution(4298696338093854765)
XLA Ops:
  0.0 1.5 %copy.13.dt_ref = bf16[256,64]{1,0:T(8,128)(2,1)} copy(bf16[256,64]{0,1:T(8,128)(2,1)} %param.15) | data formatting | bytes 65536 | tf_op args[3]
  1.5 45.1 %shard_map.118 = bf16[256,4096]{1,0:T(8,128)(2,1)} custom-call(bf16[256,4096]{1,0:T(8,128)(2,1)} %x_hbm.1, bf16[256,4096]{1,0:T(8,128)(2,1)} %z_hbm.1, bf16[256,256]{1,0:T(8,128)(2,1)} %bc_ref.1, bf16[256,64]{1,0:T(8,128)(2,1)} %copy.13.dt_ref, f32[4,4096]{1,0:T(4,128)} %wx_ref.1, f32[1,4096]{1,0:T(1,128)} %bitcast.6, f32[4,256]{1,0:T(4,128)} %wbc_ref.1, ...), custom_call_target="tpu_custom_call" | custom-call | tf_op jit(solution)/shard_map/pallas_call | solution.py:636
  46.6 3.1 %copy.15 = bf16[256,4096]{1,0:T(8,128)(2,1)} copy(bf16[256,4096]{1,0:T(8,128)(2,1)} %shard_map.118) | data formatting | bytes 4194304
where the time goes:
time: 50.4 us; the launch traced here: 49.7 us
  Pallas kernels  45.1 us (89%)
  local copies, waits for them, and re-layouts  4.62 us (9%)
    pallas_call x1, Pallas kernels, body(): pl.pallas_call(functools.partial(kernel, nz, nx, di, nk), out_shape=jax.S...  45.1 us
    unnamed x2, local copies, waits for them, and re-layouts  4.62 us

commit v1 on v0

--- a/solution.py
+++ b/solution.py
@@ -30,6 +30,17 @@
     nk,
     x_hbm,
     z_hbm,
+    bc_hbm,
+    dt_hbm,
+    wx_hbm,
+    bx_hbm,
+    wbc_hbm,
+    bbc_hbm,
+    dtb_hbm,
+    alog_hbm,
+    skip_hbm,
+    gain_hbm,
+    out_hbm,
     bc_ref,
     dt_ref,
     wx_ref,
@@ -40,13 +51,14 @@
     alog_ref,
     skip_ref,
     gain_ref,
-    out_hbm,
+    bcs,
+    zs,
     xv,
     zv,
     xc,
     halo_x,
     halo_bc,
-    dtw,
+    r2s,
     ex,
     ldg,
     rt,
@@ -81,6 +93,7 @@
     entsend,
     ent,
     sem_in,
+    sem_small,
     sem_out,
     sem_halo,
     sem_l,
@@ -134,25 +147,46 @@
             src_ref=src, dst_ref=dst, send_sem=ss, recv_sem=rs, device_id={"seq": dev}
         )
 
-    half = di // 2
-    cols = [pl.ds(0, half), pl.ds(half, half)]
-    xin = [pltpu.make_async_copy(x_hbm.at[:, q], xv.at[:, q], sem_in.at[i]) for i, q in enumerate(cols)]
-    zin = pltpu.make_async_copy(z_hbm, zv, sem_in.at[2])
-    for cp in xin:
+    def lanes_of(k):
+        return pl.ds(k * ch, ch)
+
+    smalls = [
+        (dt_hbm, dt_ref),
+        (dtb_hbm, dtb_ref),
+        (alog_hbm, alog_ref),
+        (bc_hbm, bc_ref),
+        (wx_hbm, wx_ref),
+        (bx_hbm, bx_ref),
+        (wbc_hbm, wbc_ref),
+        (bbc_hbm, bbc_ref),
+        (skip_hbm, skip_ref),
+        (gain_hbm, gain_ref),
+    ]
+    small_in = [pltpu.make_async_copy(p, q, sem_small.at[i]) for i, (p, q) in enumerate(smalls)]
+    xin = [
+        pltpu.make_async_copy(x_hbm.at[:, lanes_of(k)], xv.at[:, lanes_of(k)], sem_in.at[k])
+        for k in range(nk)
+    ]
+    zin = pltpu.make_async_copy(z_hbm, zv, sem_in.at[nk])
+    for cp in small_in[0:3]:
+        cp.start()
+    xin[0].start()
+    for cp in small_in[3:]:
+        cp.start()
+    for cp in xin[1:]:
         cp.start()
     zin.start()
 
-    dtw[:, 0:HL] = dt_ref[...].astype(F32) + dtb_ref[...]
-    dtw[:, HL : 2 * HL] = dt_ref[...].astype(F32) + dtb_ref[...]
-    lo_b[:, 0:HL] = jnp.broadcast_to(jnp.exp(alog_ref[...]), (8, HL))
-    lo_b[:, HL : 2 * HL] = jnp.broadcast_to(jnp.exp(alog_ref[...]), (8, HL))
-    arate = lo_b[0:1, :]
-    lo_b[:, 0:HL] = jnp.broadcast_to(skip_ref[...], (8, HL))
-    lo_b[:, HL : 2 * HL] = jnp.broadcast_to(skip_ref[...], (8, HL))
-    skipd = lo_b[...]
-    raw = dtw[...]
+    def twice(ref):
+        row = jnp.broadcast_to(ref[...], (8, HL))
+        return jnp.concatenate([row, row], axis=1)
+
+    for cp in small_in[0:3]:
+        cp.wait()
+    dtv = dt_ref[...].astype(F32)
+    raw = jnp.transpose(jnp.concatenate([dtv, dtv], axis=0)) + twice(dtb_ref)[0:1]
     step = jnp.maximum(raw, 0.0) + jnp.log1p(jnp.exp(-jnp.abs(raw)))
-    rate = -arate * step
+    rate = -jnp.exp(twice(alog_ref)[0:1]) * step
     low = lax.broadcasted_iota(jnp.int32, (T, T), 0) >= lax.broadcasted_iota(jnp.int32, (T, T), 1)
     ld2 = jnp.dot(
         jnp.where(low, 1.0, 0.0),
@@ -162,6 +196,8 @@
     ) * LOG2E
     r2 = ld2 - jnp.log(step) * LOG2E
     last2 = ld2[T - 1 : T, :]
+    ldg[0] = ld2
+    r2s[...] = r2
 
     def pair(v):
         hi = v.astype(BF16).astype(F32)
@@ -169,24 +205,20 @@
         return jnp.where(lane < HL, hi, v - hi).astype(BF16)
 
     f1s[...] = pair(jnp.exp2(last2 - r2))
-    f2s[...] = pair(jnp.exp2(ld2))
-    rt[...] = jnp.transpose(r2)
-    for g in range(ngroup):
-        ldg[g] = ld2 if g == 0 else pltpu.roll(ld2, 128 - 8 * g, axis=1)
     lo_b[...] = jnp.broadcast_to(last2, (8, 2 * HL))
 
-    @pl.loop(0, ngroup)
-    def _(g):
-        row = lax.broadcasted_iota(jnp.int32, (128, 512), 0) & 63
-        head = (lax.broadcasted_iota(jnp.int32, (128, 512), 1) >> 6) + g * 8
-        lanes = pl.ds(pl.multiple_of(g * 512, 512), 512)
-        ex[:, lanes] = jnp.where(row == head, 1.0, 0.0).astype(BF16)
-        skw[:, lanes] = dot(pair(jnp.concatenate([skipd, skipd], 0)), ex[:, lanes])[0:8]
+    def make_ex(k):
+        @pl.loop(0, ch // 256)
+        def _(j):
+            base = k * ch + j * 256
+            row = lax.broadcasted_iota(jnp.int32, (128, 256), 0) & 63
+            head = (lax.broadcasted_iota(jnp.int32, (128, 256), 1) + base) >> 6
+            ex[:, pl.ds(pl.multiple_of(base, 256), 256)] = jnp.where(row == head, 1.0, 0.0).astype(BF16)
 
     pl.semaphore_wait(barrier, len(peers))
     hal = [
         rcopy(x_hbm.at[pl.ds(T - 8, 8), :], halo_x, sem_halo.at[0], sem_halo.at[1], nxt),
-        rcopy(bc_ref.at[pl.ds(T - 8, 8), :], halo_bc, sem_halo.at[2], sem_halo.at[3], nxt),
+        rcopy(bc_hbm.at[pl.ds(T - 8, 8), :], halo_bc, sem_halo.at[2], sem_halo.at[3], nxt),
     ]
     for cp in hal:
         cp.start()
@@ -208,47 +240,42 @@
             acc = acc + w_ref[3 - k : 4 - k, lanes] * pltpu.roll(v, k, axis=0)
         return silu(acc[8:24]).astype(BF16)
 
-    for i in range(2):
-        xin[i].wait()
-
-        @pl.loop(0, half // 256)
+    def stage_main(k):
+        xin[k].wait()
+
+        @pl.loop(0, ch // 256)
         def _(j):
-            conv_main(xv, xc, wx_ref, bx_ref, pl.ds(pl.multiple_of(i * half + j * 256, 256), 256))
-
+            conv_main(xv, xc, wx_ref, bx_ref, pl.ds(pl.multiple_of(k * ch + j * 256, 256), 256))
+
+    def stage_head(k):
+        lanes = lanes_of(k)
+        xc[0:16, lanes] = conv_head(xv, halo_x, wx_ref, bx_ref, lanes)
+
+    whole = pl.ds(0, 2 * N)
+    make_ex(0)
+    for cp in small_in[3:]:
+        cp.wait()
+    stage_main(0)
+    conv_main(bc_ref, bcs, wbc_ref, bbc_ref, whole)
     for cp in hal:
         cp.wait_recv()
-
-    @pl.loop(0, di // 512)
-    def _(j):
-        lanes = pl.ds(pl.multiple_of(j * 512, 512), 512)
-        xc[0:16, lanes] = conv_head(xv, halo_x, wx_ref, bx_ref, lanes)
-
-    whole = pl.ds(0, 2 * N)
-    bcs = ov.at[:, pl.ds(0, 2 * N)]
-    conv_main(bc_ref, bcs, wbc_ref, bbc_ref, whole)
     bcs[0:16, :] = conv_head(bc_ref, halo_bc, wbc_ref, bbc_ref, whole)
-    bm = bcs[:, 0:N]
-    cm[...] = bcs[:, N : 2 * N]
-    bt[...] = jnp.transpose(bm.astype(F32)).astype(BF16)
-
-    lcopy.wait_recv()
-    own = lo_b[...]
-    other = lp_b[...]
+    bt[...] = jnp.transpose(bcs[:, 0:N].astype(F32)).astype(BF16)
+
     first = c == 0
-    l0 = jnp.where(first, own, other)
-    l1 = jnp.where(first, other, own)
-    cl = l0 + l1
-    cl_b[...] = cl
-    xd_b[x] = cl
-    dxs = [rcopy(cl_b, xd_b.at[x], sx_s.at[d], sx_r.at[x], at(z, xp, c)) for d, xp in enumerate(xpeer)]
-    for cp in dxs:
-        cp.start()
-    dl[...] = dot(
-        pair(jnp.concatenate([jnp.exp2(l0), jnp.exp2(l1)], axis=0)), ex[...]
-    )
-
-    def lanes_of(k):
-        return pl.ds(k * ch, ch)
+
+    def stage_decay_l():
+        lcopy.wait_recv()
+        own = lo_b[...]
+        other = lp_b[...]
+        l0 = jnp.where(first, own, other)
+        l1 = jnp.where(first, other, own)
+        cl = l0 + l1
+        cl_b[...] = cl
+        xd_b[x] = cl
+        for d, xp in enumerate(xpeer):
+            rcopy(cl_b, xd_b.at[x], sx_s.at[d], sx_r.at[x], at(z, xp, c)).start()
+        dl[...] = dot(pair(jnp.concatenate([jnp.exp2(l0), jnp.exp2(l1)], axis=0)), ex[...])
 
     oh = pl.multiple_of(c * hr, hr)
     ph = pl.multiple_of((1 - c) * hr, hr)
@@ -440,7 +467,15 @@
         db_copy(k).start()
         ent[pl.ds(oh, hr), lanes] = jnp.where(first, e0, e1)
 
-    def scores():
+    def prepare():
+        cm[...] = bcs[:, N : 2 * N]
+        base = ldg[0]
+        for g in range(1, ngroup):
+            ldg[g] = pltpu.roll(base, 128 - 8 * g, axis=1)
+        rt[...] = jnp.transpose(r2s[...])
+        f2s[...] = pair(jnp.exp2(base))
+        skipd = twice(skip_ref)
+        skw[...] = dot(pair(jnp.concatenate([skipd, skipd], 0)), ex[...])[0:8]
         s = lax.dot_general(
             cm[...], bcs[:, 0:N], (((1,), (1,)), ((), ())), preferred_element_type=F32
         )
@@ -477,6 +512,10 @@
             inside[0:hb, lanes] = yt + sk[0:hb]
             inside[hb:T, lanes] = yb + sk[hb:T]
 
+    def silu_group(g):
+        lanes = pl.ds(g * 512, 512)
+        zs[:, lanes] = silu(zv[:, lanes].astype(F32))
+
     def stage_g(k):
         db_copy(k).wait_recv()
 
@@ -485,45 +524,58 @@
             lanes = pl.ds(pl.multiple_of(k * ch + j * 256, 256), 256)
             f2e = dot(f2s[...], ex[:, lanes])
             y = (inside[:, lanes] + f2e * dot(cm[...], ent[:, lanes])).astype(BF16)
-            gated = y.astype(F32) * silu(zv[:, lanes].astype(F32))
+            gated = y.astype(F32) * zs[:, lanes]
             inside[:, lanes] = gated
             sq = gated * gated
             ssq[...] += sq[:, 0:128] + sq[:, 128:256]
 
+    fill = [functools.partial(mix_group, g) for g in range(ngroup)]
+    fill += [functools.partial(silu_group, g) for g in range(ngroup)]
+
+    def filler(n):
+        for _ in range(n):
+            if fill:
+                fill.pop(0)()
+
+    stage_head(0)
     stage_a(0)
+    for k in range(1, nk):
+        make_ex(k)
+    stage_main(1)
+    stage_head(1)
     stage_a(1)
+    stage_decay_l()
     stage_b(0)
     for k in range(2, nk):
+        stage_main(k)
+        stage_head(k)
         stage_a(k)
         stage_b(k - 1)
     stage_decay_x()
     stage_b(nk - 1)
-    scores()
+    prepare()
     ssq[...] = jnp.zeros_like(ssq)
     zin.wait()
 
-    fill = list(range(ngroup))
-
-    def filler():
-        if fill:
-            g = fill.pop(0)
-            mix_group(g)
-
     for s in range(nk):
-        filler()
         stage_c(s)
+        filler(1)
+    filler(1)
     stage_decay_z()
     for s in range(nk):
-        filler()
         stage_d(s)
-    while fill:
-        filler()
+        filler(1)
+    filler(3)
     for s in range(nk):
         stage_e(s)
-    for s in range(nk):
+        filler(1)
+    while fill:
+        filler(1)
+    stage_f(0)
+    for s in range(1, nk):
         stage_f(s)
-    for s in range(nk):
-        stage_g(s)
+        stage_g(s - 1)
+    stage_g(nk - 1)
 
     ms = jnp.sum(ssq[...], axis=1, keepdims=True) * (1.0 / di)
     rs = lax.rsqrt(ms + 1e-05)
@@ -542,8 +594,8 @@
     for cp in hal:
         cp.wait_send()
     lcopy.wait_send()
-    for d in range(nx - 1):
-        dxs[d].wait_send()
+    for d, xp in enumerate(xpeer):
+        rcopy(cl_b, xd_b.at[x], sx_s.at[d], sx_r.at[x], at(z, xp, c)).wait_send()
     for d, zp in enumerate(zpeer):
         rcopy(pl_b, zd_b.at[z], sz_s.at[d], sz_r.at[z], at(zp, x, c)).wait_send()
     for k in range(nk):
@@ -571,8 +623,19 @@
         vb = lambda *s: pltpu.VMEM(s, BF16)
         dma = lambda *s: pltpu.SemaphoreType.DMA(s)
         anyspec = pl.BlockSpec(memory_space=pl.ANY)
-        vspec = pl.BlockSpec(memory_space=pltpu.VMEM)
         scratch = [
+            vb(T, 2 * N),
+            vb(HL, T),
+            vm(4, di),
+            vm(1, di),
+            vm(4, 2 * N),
+            vm(1, 2 * N),
+            vm(1, HL),
+            vm(1, HL),
+            vm(1, HL),
+            vm(1, di),
+            vb(T, 2 * N),
+            vm(T, di),
             vb(T, di),
             vb(T, di),
             vb(T, di),
@@ -612,7 +675,8 @@
             vb(hr, di),
             vb(hr, di),
             vb(N, di),
-            dma(3),
+            dma(nk + 1),
+            dma(10),
             dma(nk),
             dma(4),
             dma(2),
@@ -636,7 +700,7 @@
         return pl.pallas_call(
             functools.partial(kernel, nz, nx, di, nk),
             out_shape=jax.ShapeDtypeStruct((T, di), BF16),
-            in_specs=[anyspec, anyspec] + [vspec] * 10,
+            in_specs=[anyspec] * 12,
             out_specs=anyspec,
             scratch_shapes=scratch,
             compiler_params=pltpu.CompilerParams(
@@ -646,7 +710,7 @@
             x_raw,
             z_gate,
             bc_raw,
-            dt_raw,
+            dt_raw.T,
             wx,
             bx.reshape(1, -1),
             wbc,

time: 50.4 us -> 49.6 us (0.984); the launches traced: 49.7 us -> 49.5 us
  local copies, waits for them, and re-layouts: 4.62 us -> 3.13 us
  Pallas kernels: 45.1 us -> 46.3 us
    unnamed x2 -> x1, local copies, waits for them, and re-layouts: 4.62 us -> 3.13 us
    pallas_call x1, Pallas kernels: 45.1 us -> 46.3 us  [body(): pl.pallas_call(functools.partial(kernel, nz, nx, di, nk), out_shape=jax.S...]
where the time goes in v1:
time: 49.6 us; the launch traced here: 49.5 us
  Pallas kernels  46.3 us (93%)
  local copies, waits for them, and re-layouts  3.13 us (6%)
    pallas_call x1, Pallas kernels, body(): pl.pallas_call(functools.partial(kernel, nz, nx, di, nk), out_shape=jax.S...  46.3 us
    unnamed x1, local copies, waits for them, and re-layouts  3.13 us

profile of v1, /device:TPU:1, one launch (start us, length us, event | category | flops | bytes accessed | tf_op | source)
XLA Modules:
  0.0 49.5 jit_solution(6937174646927843451)
XLA Ops:
  0.0 46.3 %shard_map.118 = bf16[256,4096]{1,0:T(8,128)(2,1)} custom-call(bf16[256,4096]{1,0:T(8,128)(2,1)} %x_hbm.1, bf16[256,4096]{1,0:T(8,128)(2,1)} %z_hbm.1, bf16[256,256]{1,0:T(8,128)(2,1)} %bc_hbm.1, bf16[64,256]{1,0:T(8,128)(2,1)} %bitcast.7, f32[4,4096]{1,0:T(4,128)} %wx_hbm.1, f32[1,4096]{1,0:T(1,128)} %bitcast.8, f32[4,256]{1,0:T(4,128)} %wbc_hbm.1, ...), custom_call_target="tpu_custom_call" | custom-call | tf_op jit(solution)/shard_map/pallas_call | solution.py:700
  46.4 3.1 %copy.14 = bf16[256,4096]{1,0:T(8,128)(2,1)} copy(bf16[256,4096]{1,0:T(8,128)(2,1)} %shard_map.118) | data formatting | bytes 4194304

commit v2 on v1

--- a/solution.py
+++ b/solution.py
@@ -28,6 +28,7 @@
     nx,
     di,
     nk,
+    no,
     x_hbm,
     z_hbm,
     bc_hbm,
@@ -39,8 +40,8 @@
     dtb_hbm,
     alog_hbm,
     skip_hbm,
-    gain_hbm,
-    out_hbm,
+    inside,
+    rs_ref,
     bc_ref,
     dt_ref,
     wx_ref,
@@ -50,7 +51,6 @@
     dtb_ref,
     alog_ref,
     skip_ref,
-    gain_ref,
     bcs,
     zs,
     xv,
@@ -68,9 +68,7 @@
     cm,
     sc,
     skw,
-    inside,
     ssq,
-    ov,
     lo_b,
     lp_b,
     cl_b,
@@ -94,7 +92,6 @@
     ent,
     sem_in,
     sem_small,
-    sem_out,
     sem_halo,
     sem_l,
     sx_s,
@@ -115,7 +112,7 @@
     db_r,
 ):
     ch = di // nk
-    zw = ch // nz
+    zw = ch // no
     hr = N // 2
     xr = hr // nx
     ngroup = di // 512
@@ -160,7 +157,6 @@
         (wbc_hbm, wbc_ref),
         (bbc_hbm, bbc_ref),
         (skip_hbm, skip_ref),
-        (gain_hbm, gain_ref),
     ]
     small_in = [pltpu.make_async_copy(p, q, sem_small.at[i]) for i, (p, q) in enumerate(smalls)]
     xin = [
@@ -257,6 +253,14 @@
         cp.wait()
     stage_main(0)
     conv_main(bc_ref, bcs, wbc_ref, bbc_ref, whole)
+    make_ex(1)
+    stage_main(1)
+    stage_main(2 % nk) if nk > 2 else None
+
+    @pl.when(z == 0)
+    def _():
+        perecv[...] = jnp.zeros_like(perecv)
+
     for cp in hal:
         cp.wait_recv()
     bcs[0:16, :] = conv_head(bc_ref, halo_bc, wbc_ref, bbc_ref, whole)
@@ -326,6 +330,9 @@
         for d in range(nx - 1):
             x_copy(k, d).start()
         xrecv[x, :, lanes] = csb[pl.ds(pl.multiple_of(x * xr, xr), xr), lanes]
+
+    def zd_copy(o):
+        return rcopy(pl_b, zd_b.at[z], sz_s.at[o], sz_r.at[z], at(o, x, c))
 
     def stage_decay_x():
         for d, xp in enumerate(xpeer):
@@ -344,26 +351,29 @@
         )
         dx[...] = dot(pair(jnp.exp2(full)), ex[...])
         pl_b[...] = jnp.broadcast_to(total, (8, 2 * HL))
-        zd_b[z] = jnp.broadcast_to(total, (8, 2 * HL))
-        for d, zp in enumerate(zpeer):
-            rcopy(pl_b, zd_b.at[z], sz_s.at[d], sz_r.at[z], at(zp, x, c)).start()
-
-    def stage_decay_z():
-        for d, zp in enumerate(zpeer):
-            rcopy(pl_b, zd_b.at[zp], sz_s.at[d], sz_r.at[zp], at(zp, x, c)).wait_recv()
-        full = jnp.concatenate(
-            [zd_b[i][0:1] for i in range(nz)] + [jnp.zeros((16 - nz, 2 * HL), F32)], axis=0
-        )
-        full = pair(jnp.exp2(full))
-        for k in range(nk):
-            lanes = pl.ds(pl.multiple_of(k * ch + z * zw, zw), zw)
-            dz[:, k * zw : (k + 1) * zw] = dot(full, ex[:, lanes])
-
-    def z_copy(k, d):
-        zp = zpeer[d]
-        src = ptb.at[:, pl.ds(pl.multiple_of(k * ch + zp * zw, zw), zw)]
+        for o in range(no):
+
+            @pl.when(z == o)
+            def _():
+                zd_b[o] = jnp.broadcast_to(total, (8, 2 * HL))
+
+            @pl.when((z != o) & (z < nz - 1))
+            def _():
+                zd_copy(o).start()
+
+    def own_lanes(k):
+        return pl.ds(k * zw, zw)
+
+    def lanes_to(k, o):
+        return pl.ds(k * ch + o * zw, zw)
+
+    def z_copy(k, o):
         return rcopy(
-            src, zrecv.at[z, :, pl.ds(k * zw, zw)], z_s.at[k, d], z_r.at[k, z], at(zp, x, c)
+            ptb.at[:, lanes_to(k, o)],
+            zrecv.at[z, :, own_lanes(k)],
+            z_s.at[k, o],
+            z_r.at[k, z],
+            at(o, x, c),
         )
 
     def stage_c(k):
@@ -374,38 +384,61 @@
         for i in range(1, nx):
             tot = tot + dx[i : i + 1, lanes] * xrecv[i, :, lanes].astype(F32)
         ptb[:, lanes] = tot.astype(BF16)
-        for d in range(nz - 1):
-            z_copy(k, d).start()
-        zrecv[z, :, pl.ds(k * zw, zw)] = ptb[:, pl.ds(pl.multiple_of(k * ch + z * zw, zw), zw)]
-
-    def zb_copy(k, d):
-        zp = zpeer[d]
-        lanes = pl.ds(pl.multiple_of(k * ch + z * zw, zw), zw)
+        for o in range(no):
+
+            @pl.when(z == o)
+            def _():
+                zrecv[o, :, own_lanes(k)] = ptb[:, lanes_to(k, o)]
+
+            @pl.when((z != o) & (z < nz - 1))
+            def _():
+                z_copy(k, o).start()
+
+    def zb_copy(k, o, j):
         return rcopy(
-            pesend.at[zp, :, pl.ds(k * zw, zw)],
-            perecv.at[:, lanes],
-            zb_s.at[k, d],
-            zb_r.at[k, z],
-            at(zp, x, c),
-        )
-
-    def stage_d(k):
-        own_lanes = pl.ds(k * zw, zw)
-        for d, zp in enumerate(zpeer):
-            rcopy(
-                ptb.at[:, pl.ds(0, zw)],
-                zrecv.at[zp, :, own_lanes],
-                z_s.at[k, d],
-                z_r.at[k, zp],
-                at(zp, x, c),
-            ).wait_recv()
-        state = jnp.zeros((xr, zw), F32)
-        for i in range(nz):
-            pesend[i, :, own_lanes] = state.astype(BF16)
-            state = dz[i : i + 1, own_lanes] * state + zrecv[i, :, own_lanes].astype(F32)
-        for d in range(nz - 1):
-            zb_copy(k, d).start()
-        perecv[:, pl.ds(pl.multiple_of(k * ch + z * zw, zw), zw)] = pesend[z, :, own_lanes]
+            pesend.at[j, :, own_lanes(k)],
+            perecv.at[:, lanes_to(k, o)],
+            zb_s.at[k, j],
+            zb_r.at[k, o],
+            at(j, x, c),
+        )
+
+    def stage_d():
+        lead = [0.0, 1.5, 2.7, 3.5, 4.3, 4.6, 4.8, 5.0]
+        order = sorted(
+            (lead[min(i, 7)] + 1.1 * k, i, k) for i in range(nz - 1) for k in range(nk)
+        )
+        for o in range(no):
+
+            @pl.when(z == o)
+            def _():
+                states = [jnp.zeros((xr, zw), F32) for _ in range(nk)]
+                seen = []
+                for _, i, k in order:
+                    if i not in seen:
+                        seen.append(i)
+                        if i != o:
+                            rcopy(pl_b, zd_b.at[i], sz_s.at[0], sz_r.at[i], at(i, x, c)).wait_recv()
+                        e = jnp.exp2(zd_b[i])
+                        full = pair(jnp.concatenate([e, e], axis=0))
+                        for q in range(nk):
+                            dz[i, :, q * zw : (q + 1) * zw] = dot(full, ex[:, lanes_to(q, o)])
+                    if i != o:
+                        rcopy(
+                            ptb.at[:, pl.ds(0, zw)],
+                            zrecv.at[i, :, own_lanes(k)],
+                            z_s.at[k, 0],
+                            z_r.at[k, i],
+                            at(i, x, c),
+                        ).wait_recv()
+                    old = states[k]
+                    new = dz[i, 0:1, own_lanes(k)] * old + zrecv[i, :, own_lanes(k)].astype(F32)
+                    states[k] = new
+                    if i + 1 == o:
+                        perecv[:, lanes_to(k, o)] = new.astype(BF16)
+                    else:
+                        pesend[i + 1, :, own_lanes(k)] = new.astype(BF16)
+                        zb_copy(k, o, i + 1).start()
 
     def xb_copy(k, d):
         xp = xpeer[d]
@@ -419,15 +452,18 @@
         )
 
     def stage_e(k):
-        for d, zp in enumerate(zpeer):
-            lanes = pl.ds(pl.multiple_of(k * ch + zp * zw, zw), zw)
-            rcopy(
-                pesend.at[zp, :, pl.ds(k * zw, zw)],
-                perecv.at[:, lanes],
-                zb_s.at[k, d],
-                zb_r.at[k, zp],
-                at(zp, x, c),
-            ).wait_recv()
+        for o in range(no):
+
+            @pl.when((z != o) & (z > 0))
+            def _():
+                rcopy(
+                    pesend.at[0, :, own_lanes(k)],
+                    perecv.at[:, lanes_to(k, o)],
+                    zb_s.at[k, 0],
+                    zb_r.at[k, o],
+                    at(o, x, c),
+                ).wait_recv()
+
         lanes = lanes_of(k)
         state = perecv[:, lanes].astype(F32)
         for i in range(nx):
@@ -539,15 +575,15 @@
 
     stage_head(0)
     stage_a(0)
-    for k in range(1, nk):
-        make_ex(k)
-    stage_main(1)
     stage_head(1)
     stage_a(1)
+    for k in range(2, nk):
+        make_ex(k)
     stage_decay_l()
     stage_b(0)
     for k in range(2, nk):
-        stage_main(k)
+        if k > 2:
+            stage_main(k)
         stage_head(k)
         stage_a(k)
         stage_b(k - 1)
@@ -560,17 +596,11 @@
     for s in range(nk):
         stage_c(s)
         filler(1)
-    filler(1)
-    stage_decay_z()
-    for s in range(nk):
-        stage_d(s)
+    while fill:
         filler(1)
-    filler(3)
+    stage_d()
     for s in range(nk):
         stage_e(s)
-        filler(1)
-    while fill:
-        filler(1)
     stage_f(0)
     for s in range(1, nk):
         stage_f(s)
@@ -578,51 +608,70 @@
     stage_g(nk - 1)
 
     ms = jnp.sum(ssq[...], axis=1, keepdims=True) * (1.0 / di)
-    rs = lax.rsqrt(ms + 1e-05)
-    outs = []
-    for i in range(nk):
-
-        @pl.loop(0, ch // 256)
-        def _(j):
-            lanes = pl.ds(pl.multiple_of(i * ch + j * 256, 256), 256)
-            ov[:, lanes] = (inside[:, lanes] * rs * gain_ref[:, lanes]).astype(BF16)
-
-        cp = pltpu.make_async_copy(ov.at[:, lanes_of(i)], out_hbm.at[:, lanes_of(i)], sem_out.at[i])
-        cp.start()
-        outs.append(cp)
+    rs_ref[...] = jnp.broadcast_to(lax.rsqrt(ms + 1e-05), (T, 128))
 
     for cp in hal:
         cp.wait_send()
     lcopy.wait_send()
     for d, xp in enumerate(xpeer):
         rcopy(cl_b, xd_b.at[x], sx_s.at[d], sx_r.at[x], at(z, xp, c)).wait_send()
-    for d, zp in enumerate(zpeer):
-        rcopy(pl_b, zd_b.at[z], sz_s.at[d], sz_r.at[z], at(zp, x, c)).wait_send()
+    for o in range(no):
+
+        @pl.when((z != o) & (z < nz - 1))
+        def _():
+            zd_copy(o).wait_send()
+            for k in range(nk):
+                z_copy(k, o).wait_send()
+
+        @pl.when(z == o)
+        def _():
+            for k in range(nk):
+                for j in range(1, nz):
+                    if j != o:
+                        zb_copy(k, o, j).wait_send()
+
     for k in range(nk):
         d_copy(k).wait_send()
         db_copy(k).wait_send()
         for d in range(nx - 1):
             x_copy(k, d).wait_send()
             xb_copy(k, d).wait_send()
-        for d in range(nz - 1):
-            z_copy(k, d).wait_send()
-            zb_copy(k, d).wait_send()
-    for cp in outs:
-        cp.wait()
-
-
-def make_body(nz, nx, nk):
+
+
+def norm_kernel(gated, scale, gain_hbm, out_hbm, ov, gain, sem_in, sem_out):
+    di = gated.shape[1]
+    quarter = di // 4
+    cp = pltpu.make_async_copy(gain_hbm, gain, sem_in.at[0])
+    cp.start()
+    cp.wait()
+    outs = []
+    for i in range(4):
+
+        @pl.loop(0, quarter // 128)
+        def _(j):
+            lanes = pl.ds(pl.multiple_of(i * quarter + j * 128, 128), 128)
+            ov[:, lanes] = (gated[:, lanes] * scale[...] * gain[:, lanes]).astype(BF16)
+
+        lanes = pl.ds(i * quarter, quarter)
+        out = pltpu.make_async_copy(ov.at[:, lanes], out_hbm.at[:, lanes], sem_out.at[i])
+        out.start()
+        outs.append(out)
+    for out in outs:
+        out.wait()
+
+
+def make_body(nz, nx, nk, no):
     def body(x_raw, z_gate, bc_raw, dt_raw, wx, bx, wbc, bbc, dtb, alog, skip, gain):
         di = x_raw.shape[1]
         ch = di // nk
-        zw = ch // nz
+        zw = ch // no
         hr = N // 2
         xr = hr // nx
         ng = di // 512
         vm = lambda *s: pltpu.VMEM(s, F32)
         vb = lambda *s: pltpu.VMEM(s, BF16)
         dma = lambda *s: pltpu.SemaphoreType.DMA(s)
-        anyspec = pl.BlockSpec(memory_space=pl.ANY)
+        anyspec = pl.BlockSpec(memory_space=pltpu.HBM)
         scratch = [
             vb(T, 2 * N),
             vb(HL, T),
@@ -633,7 +682,6 @@
             vm(1, HL),
             vm(1, HL),
             vm(1, HL),
-            vm(1, di),
             vb(T, 2 * N),
             vm(T, di),
             vb(T, di),
@@ -651,9 +699,7 @@
             vb(T, N),
             vm(T, T),
             vm(8, di),
-            vm(T, di),
             vm(T, 128),
-            vb(T, di),
             vm(8, 128),
             vm(8, 128),
             vm(8, 128),
@@ -662,7 +708,7 @@
             vm(nz, 8, 128),
             vm(16, di),
             vm(16, di),
-            vm(16, nk * zw),
+            vm(nz, 16, nk * zw),
             vb(N, di),
             vb(hr, di),
             vb(hr, di),
@@ -676,8 +722,7 @@
             vb(hr, di),
             vb(N, di),
             dma(nk + 1),
-            dma(10),
-            dma(nk),
+            dma(9),
             dma(4),
             dma(2),
             dma(nx),
@@ -697,16 +742,22 @@
             dma(nk),
             dma(nk),
         ]
-        return pl.pallas_call(
-            functools.partial(kernel, nz, nx, di, nk),
-            out_shape=jax.ShapeDtypeStruct((T, di), BF16),
-            in_specs=[anyspec] * 12,
-            out_specs=anyspec,
+        gated, scale = pl.pallas_call(
+            functools.partial(kernel, nz, nx, di, nk, no),
+            out_shape=(
+                pltpu.VMEM((T, di), F32),
+                pltpu.VMEM((T, 128), F32),
+            ),
+            in_specs=[anyspec] * 11,
+            out_specs=(pl.BlockSpec(memory_space=pltpu.VMEM),) * 2,
             scratch_shapes=scratch,
             compiler_params=pltpu.CompilerParams(
-                collective_id=0, has_side_effects=True, vmem_limit_bytes=60 * 1024 * 1024
+                collective_id=0, has_side_effects=True, vmem_limit_bytes=48 * 1024 * 1024
             ),
         )(
+            *(
+                pltpu.with_memory_space_constraint(a, pltpu.HBM)
+                for a in (
             x_raw,
             z_gate,
             bc_raw,
@@ -718,8 +769,18 @@
             dtb.reshape(1, -1),
             alog.reshape(1, -1),
             skip.reshape(1, -1),
-            gain.reshape(1, -1),
-        )
+                )
+            )
+        )
+        full = pl.BlockSpec(memory_space=pltpu.VMEM)
+        return pl.pallas_call(
+            norm_kernel,
+            out_shape=jax.ShapeDtypeStruct((T, di), BF16),
+            in_specs=[full, full, anyspec],
+            out_specs=anyspec,
+            scratch_shapes=[vb(T, di), vm(1, di), dma(1), dma(4)],
+            compiler_params=pltpu.CompilerParams(vmem_limit_bytes=16 * 1024 * 1024),
+        )(gated, scale, pltpu.with_memory_space_constraint(gain.reshape(1, -1), pltpu.HBM))
 
     return body
 
@@ -729,7 +790,7 @@
     nz = mesh.shape["seq"] // (2 * nx)
     tok = P(("vol", "seq"), None)
     return jax.shard_map(
-        make_body(nz, nx, 4),
+        make_body(nz, nx, 4, 2),
         mesh=mesh,
         in_specs=(tok, tok, tok, tok) + (P(),) * 8,
         out_specs=tok,

time: 49.6 us -> 47.2 us (0.952)
  the two profiles are of different devices: /device:TPU:1 before, /device:TPU:169 now
where the time goes in v2:
time: 47.2 us; the launch traced here: 47 us
  Pallas kernels  47 us (100%)
    pallas_call x1, Pallas kernels, body(): pl.pallas_call(functools.partial(kernel, nz, nx, di, nk, no), out_shape=(...  44.5 us
    pallas_call x1, Pallas kernels, body(): pl.pallas_call(norm_kernel, out_shape=jax.ShapeDtypeStruct((T, di), BF16)...  2.47 us

profile of v2, /device:TPU:169, one launch (start us, length us, event | category | flops | bytes accessed | tf_op | source)
XLA Modules:
  0.0 47.0 jit_solution(17895790684557041731)
XLA Ops:
  0.0 44.5 %shard_map.118 = (f32[256,4096]{1,0:T(8,128)S(1)}, f32[256,128]{1,0:T(8,128)S(1)}) custom-call(bf16[256,4096]{1,0:T(8,128)(2,1)} %x_hbm.1, bf16[256,4096]{1,0:T(8,128)(2,1)} %z_hbm.1, bf16[256,256]{1,0:T(8,128)(2,1)} %bc_hbm.1, bf16[64,256]{1,0:T(8,128)(2,1)} %bitcast.7, f32[4,4096]{1,0:T(4,128)} %wx_hbm.1, f32[1,4096]{1,0:T(1,128)} %bitcast.8, ...), custom_call_target="tpu_custom_call" | custom-call | tf_op jit(solution)/shard_map/pallas_call | solution.py:745
  44.5 2.5 %shard_map.119 = bf16[256,4096]{1,0:T(8,128)(2,1)} custom-call(f32[256,4096]{1,0:T(8,128)S(1)} %get-tuple-element.7.gated, f32[256,128]{1,0:T(8,128)S(1)} %get-tuple-element.8.scale, f32[1,4096]{1,0:T(1,128)} %bitcast.9), custom_call_target="tpu_custom_call" | custom-call | tf_op jit(solution)/shard_map/pallas_call | solution.py:776

commit v3 on v2

--- a/solution.py
+++ b/solution.py
@@ -404,7 +404,7 @@
         )
 
     def stage_d():
-        lead = [0.0, 1.5, 2.7, 3.5, 4.3, 4.6, 4.8, 5.0]
+        lead = [0.0, 0.8, 1.6, 2.5, 4.0, 4.0, 4.1, 4.1]
         order = sorted(
             (lead[min(i, 7)] + 1.1 * k, i, k) for i in range(nz - 1) for k in range(nk)
         )
@@ -413,16 +413,16 @@
             @pl.when(z == o)
             def _():
                 states = [jnp.zeros((xr, zw), F32) for _ in range(nk)]
-                seen = []
+                rows = []
+                for i in range(nz - 1):
+                    if i != o:
+                        rcopy(pl_b, zd_b.at[i], sz_s.at[0], sz_r.at[i], at(i, x, c)).wait_recv()
+                    rows.append(zd_b[i][0:1])
+                full = jnp.concatenate(rows + [rows[0]] * (17 - nz), axis=0)
+                full = pair(jnp.exp2(full))
+                for q in range(nk):
+                    dz[:, q * zw : (q + 1) * zw] = dot(full, ex[:, lanes_to(q, o)])
                 for _, i, k in order:
-                    if i not in seen:
-                        seen.append(i)
-                        if i != o:
-                            rcopy(pl_b, zd_b.at[i], sz_s.at[0], sz_r.at[i], at(i, x, c)).wait_recv()
-                        e = jnp.exp2(zd_b[i])
-                        full = pair(jnp.concatenate([e, e], axis=0))
-                        for q in range(nk):
-                            dz[i, :, q * zw : (q + 1) * zw] = dot(full, ex[:, lanes_to(q, o)])
                     if i != o:
                         rcopy(
                             ptb.at[:, pl.ds(0, zw)],
@@ -432,7 +432,7 @@
                             at(i, x, c),
                         ).wait_recv()
                     old = states[k]
-                    new = dz[i, 0:1, own_lanes(k)] * old + zrecv[i, :, own_lanes(k)].astype(F32)
+                    new = dz[i : i + 1, own_lanes(k)] * old + zrecv[i, :, own_lanes(k)].astype(F32)
                     states[k] = new
                     if i + 1 == o:
                         perecv[:, lanes_to(k, o)] = new.astype(BF16)
@@ -596,9 +596,10 @@
     for s in range(nk):
         stage_c(s)
         filler(1)
+    filler(6)
+    stage_d()
     while fill:
         filler(1)
-    stage_d()
     for s in range(nk):
         stage_e(s)
     stage_f(0)
@@ -708,7 +709,7 @@
             vm(nz, 8, 128),
             vm(16, di),
             vm(16, di),
-            vm(nz, 16, nk * zw),
+            vm(16, nk * zw),
             vb(N, di),
             vb(hr, di),
             vb(hr, di),
@@ -790,7 +791,7 @@
     nz = mesh.shape["seq"] // (2 * nx)
     tok = P(("vol", "seq"), None)
     return jax.shard_map(
-        make_body(nz, nx, 4, 2),
+        make_body(nz, nx, 4, 4),
         mesh=mesh,
         in_specs=(tok, tok, tok, tok) + (P(),) * 8,
         out_specs=tok,

time: 47.2 us -> 45.6 us (0.966)
  the two profiles are of different devices: /device:TPU:169 before, /device:TPU:1 now
where the time goes in v3:
time: 45.6 us; the launch traced here: 45.4 us
  Pallas kernels  45.2 us (99%)
    pallas_call x1, Pallas kernels, body(): pl.pallas_call(functools.partial(kernel, nz, nx, di, nk, no), out_shape=(...  42.8 us
    pallas_call x1, Pallas kernels, body(): pl.pallas_call(norm_kernel, out_shape=jax.ShapeDtypeStruct((T, di), BF16)...  2.47 us

profile of v3, /device:TPU:1, one launch (start us, length us, event | category | flops | bytes accessed | tf_op | source)
XLA Modules:
  0.0 45.4 jit_solution(10639528562733211587)
XLA Ops:
  0.0 42.8 %shard_map.118 = (f32[256,4096]{1,0:T(8,128)S(1)}, f32[256,128]{1,0:T(8,128)S(1)}) custom-call(bf16[256,4096]{1,0:T(8,128)(2,1)} %x_hbm.1, bf16[256,4096]{1,0:T(8,128)(2,1)} %z_hbm.1, bf16[256,256]{1,0:T(8,128)(2,1)} %bc_hbm.1, bf16[64,256]{1,0:T(8,128)(2,1)} %bitcast.7, f32[4,4096]{1,0:T(4,128)} %wx_hbm.1, f32[1,4096]{1,0:T(1,128)} %bitcast.8, ...), custom_call_target="tpu_custom_call" | custom-call | tf_op jit(solution)/shard_map/pallas_call | solution.py:746
  42.8 2.5 %shard_map.119 = bf16[256,4096]{1,0:T(8,128)(2,1)} custom-call(f32[256,4096]{1,0:T(8,128)S(1)} %get-tuple-element.7.gated, f32[256,128]{1,0:T(8,128)S(1)} %get-tuple-element.8.scale, f32[1,4096]{1,0:T(1,128)} %bitcast.9), custom_call_target="tpu_custom_call" | custom-call | tf_op jit(solution)/shard_map/pallas_call | solution.py:777
